TPU v7x, 32 devices: a whole 2x2x4 slice. The times are simulated.
32 devices in a mesh: ctx: 4 (over z), head: 4 (over y, core), rep: 2 (over x).
Axes of the slice: x: 2, y: 2, z: 4, core: 2. Of those that a mesh axis runs over, the one named last changes fastest.
Arguments:
- queries: bfloat16 [4096, 1024], P(('rep', 'ctx'), 'head'), parts along dimension 0, may hold values from -140 to 140, as said below
- key_rows: bfloat16 [4096, 256], P(('rep', 'ctx')), parts along dimension 0, may hold values from -4 to 4
- value_rows: bfloat16 [4096, 256], P(('rep', 'ctx')), parts along dimension 0, may hold values from -6 to 6
- saved_output: bfloat16 [4096, 1024], P(('rep', 'ctx'), 'head'), parts along dimension 0, may hold values from -2 to 2
- out_grad: bfloat16 [4096, 1024], P(('rep', 'ctx'), 'head'), parts along dimension 0, may hold values from -6 to 6
- block_pairs: int32 [80, 2], replicated, may hold values from -1 to 15, as said below
- piece_order: int32 [8], replicated, may hold values from 0 to 7, each once
Outputs:
- query_grad: bfloat16 [4096, 1024], P(('rep', 'ctx'), 'head'), parts along dimension 0
- key_grad: float32 [4096, 256], P(('rep', 'ctx', 'head')), parts along dimension 0
- value_grad: float32 [4096, 256], P(('rep', 'ctx', 'head')), parts along dimension 0
There are 2 independent parts, one for each index of `rep`. A program takes and returns all parts, laid end to end along the dimension named above; an argument that names none is the same for every part. Nothing has to cross between parts.
Inputs may be any that keep to these rules, and one draw needn't show every extreme that they name: `queries`: most entries are of order one; in some draws a few rows have entries up to about 60 in magnitude. `block_pairs`: each row names a query block and a key block of the 16 blocks, the key block never after the query block, or is (-1, -1) and names nothing; no pair appears twice; every query block has its diagonal pair.
All inputs are finite; a program needn't handle non-finite values.
Results may differ from a plain program's by a relative error of at most 0.0048.
Values may be sent and summed in bfloat16 or wider, within the bound.
A program may use at most 64 MiB of HBM per device.

v0:
```python
import functools

import jax
import jax.numpy as jnp
from jax import lax
from jax.experimental import pallas as pl
from jax.experimental.pallas import tpu as pltpu
from jax.sharding import PartitionSpec as P

HD = 128
BLOCK = 128
CHUNK = 32

very_low = -1e30
far = 1e9
MESH = pl.DeviceIdType.MESH
f32 = jnp.float32
bf16 = jnp.bfloat16


def kernel(
    C, G, KV, keep,
    q_ref, k_ref, v_ref, o_ref, g_ref, pairs_ref, order_ref,
    dq_ref, dk_ref, dv_ref,
    qst, dost, kv_all, sm, dp, pb, ds_all, diff, thr, part, fromsib, comb, recv,
    zsend, zrecv, fsend, frecv, sibsend, sibrecv, rsend, rrecv,
):
    rows = q_ref.shape[0]
    heads = q_ref.shape[1] // HD
    cols = rows * heads
    half = rows // G
    H = G * KV
    piece = rows // 2
    qrow = rows // H
    blocks = rows // BLOCK
    scale = HD ** -0.5
    c = lax.axis_index("ctx")
    h = lax.axis_index("head")
    g = h // G
    s = h % G
    sib = g * G + (1 - s)

    barrier = pltpu.get_barrier_semaphore()
    for gg in range(KV):
        def hail(i, _, gg=gg):
            pl.semaphore_signal(
                barrier, inc=1,
                device_id={"ctx": (c + i) % C, "head": ((g + gg) % KV) * G + s},
                device_id_type=MESH,
            )
            return 0
        lax.fori_loop(1 if gg == 0 else 0, C, hail, 0)
    pl.semaphore_signal(barrier, inc=1, device_id={"head": sib}, device_id_type=MESH)

    gcol = pl.ds(pl.multiple_of(g * HD, HD), HD)
    for i in range(G):
        kv_all[c, 0, i] = k_ref[i * half:(i + 1) * half, gcol]
        kv_all[c, 1, i] = v_ref[i * half:(i + 1) * half, gcol]

    pl.semaphore_wait(barrier, KV * C)

    def zcopy(kind, group, to):
        return pltpu.make_async_remote_copy(
            src_ref=kv_all.at[group, kind, s], dst_ref=kv_all.at[group, kind, s],
            send_sem=zsend.at[kind * C + to], recv_sem=zrecv.at[kind * C + group],
            device_id={"ctx": to}, device_id_type=MESH,
        )

    def fcopy(kind, group, part_id):
        return pltpu.make_async_remote_copy(
            src_ref=kv_all.at[group, kind, part_id], dst_ref=kv_all.at[group, kind, part_id],
            send_sem=fsend.at[kind * C + group], recv_sem=frecv.at[kind * C + group],
            device_id={"head": sib}, device_id_type=MESH,
        )

    for kind in range(2):
        def send(i, _, kind=kind):
            zcopy(kind, c, (c + i) % C).start()
            return 0
        lax.fori_loop(1, C, send, 0)

    for i in range(heads):
        qst[i * rows:(i + 1) * rows, :] = q_ref[:, i * HD:(i + 1) * HD]
        dost[i * rows:(i + 1) * rows, :] = g_ref[:, i * HD:(i + 1) * HD]

    lane = lax.broadcasted_iota(jnp.int32, (1, cols), 1) % rows
    qblk = (
        jnp.where(lane < piece, order_ref[2 * c], order_ref[2 * c + 1]) * (piece // BLOCK)
        + (lane % piece) // BLOCK
    )
    slots = C * blocks
    per_piece = piece // BLOCK
    slot_row = lax.broadcasted_iota(jnp.int32, (1, slots), 1)
    slot_col = lax.broadcasted_iota(jnp.int32, (slots, 1), 0)
    kblk_row = jnp.zeros((1, slots), jnp.int32)
    kblk_col = jnp.zeros((slots, 1), jnp.int32)
    for i in range(2 * C):
        first = order_ref[i] * per_piece
        kblk_row = jnp.where(slot_row // per_piece == i, first + slot_row % per_piece, kblk_row)
        kblk_col = jnp.where(slot_col // per_piece == i, first + slot_col % per_piece, kblk_col)
    hits_q = (pairs_ref[:, 0:1] == qblk).astype(f32)
    hits_k = (pairs_ref[:, 1:2] == kblk_row).astype(f32)
    live = lax.dot_general(hits_k, hits_q, (((0,), (0,)), ((), ())), preferred_element_type=f32)
    thr[...] = jnp.where(
        live > 0.5,
        jnp.where(kblk_col < qblk, far, jnp.where(kblk_col == qblk, 0.0, -far)),
        -far,
    ).reshape(slots, 1, cols)
    diff[...] = (
        lax.broadcasted_iota(jnp.int32, (BLOCK, BLOCK), 0)
        - lax.broadcasted_iota(jnp.int32, (BLOCK, BLOCK), 1)
    ).astype(f32)

    delta_parts = []
    for i in range(heads):
        hc = slice(i * HD, (i + 1) * HD)
        prod = g_ref[:, hc].astype(f32) * o_ref[:, hc].astype(f32)
        delta_parts.append(jnp.sum(prod.T, axis=0, keepdims=True))
    delta = jnp.concatenate(delta_parts, axis=1)

    per_block = BLOCK // CHUNK
    chunks = rows // CHUNK
    nt = (((1,), (1,)), ((), ()))

    def scores_of(group, slot):
        sm[slot] = lax.dot_general(
            kv_all[group, 0].reshape(rows, HD), qst[...], nt, preferred_element_type=f32
        )

        def mask_chunk(i, top):
            at = pl.ds(pl.multiple_of(i * CHUNK, CHUNK), CHUNK)
            local = pl.multiple_of((i % per_block) * CHUNK, CHUNK)
            away = jnp.concatenate([diff[pl.ds(local, CHUNK), :]] * (cols // BLOCK), axis=1)
            limit = thr[group * blocks + i // per_block]
            masked = jnp.where(away <= limit, sm[slot, at, :] * scale, very_low)
            sm[slot, at, :] = masked
            return jnp.maximum(top, jnp.max(masked.reshape(CHUNK // 8, 8, cols), axis=0))

        return lax.fori_loop(
            0, chunks, mask_chunk, jnp.full((8, cols), very_low, f32), unroll=2
        )

    def slot_of(group):
        return group if keep else 0

    def stats(group, carry):
        run_max, run_sum = carry
        slot = slot_of(group)
        top = jnp.max(scores_of(group, slot), axis=0, keepdims=True)
        new_max = jnp.maximum(run_max, top)

        def sum_chunk(i, total):
            at = pl.ds(pl.multiple_of(i * CHUNK, CHUNK), CHUNK)
            terms = jnp.exp(sm[slot, at, :] - new_max)
            return total + jnp.sum(terms.reshape(CHUNK // 8, 8, cols), axis=0)

        total = lax.fori_loop(0, chunks, sum_chunk, jnp.zeros((8, cols), f32), unroll=2)
        return new_max, run_sum * jnp.exp(run_max - new_max) + jnp.sum(total, axis=0, keepdims=True)

    carry = stats(c, (jnp.full((1, cols), very_low, f32), jnp.zeros((1, cols), f32)))

    def gather_step(i, carry):
        group = (c - i + C) % C
        zcopy(0, group, c).wait_recv()
        fcopy(0, group, s).start()
        fcopy(0, group, 1 - s).wait_recv()
        return stats(group, carry)

    run_max, run_sum = lax.fori_loop(1, C, gather_step, carry)
    lse = run_max + jnp.log(run_sum)

    def forward_values(i, _):
        group = (c - i + C) % C
        zcopy(1, group, c).wait_recv()
        fcopy(1, group, s).start()
        return 0

    lax.fori_loop(1, C, forward_values, 0)

    def sib_copy(group):
        return pltpu.make_async_remote_copy(
            src_ref=part.at[group, 1 - s], dst_ref=fromsib.at[group],
            send_sem=sibsend.at[group], recv_sem=sibrecv.at[group],
            device_id={"head": sib}, device_id_type=MESH,
        )

    def out_copy(group, gg, src):
        return pltpu.make_async_remote_copy(
            src_ref=comb.at[group, gg], dst_ref=recv.at[src],
            send_sem=rsend.at[group * KV + gg], recv_sem=rrecv.at[src],
            device_id={"ctx": group, "head": gg * G + s}, device_id_type=MESH,
        )

    me = c * KV + g

    def grads(group):
        slot = slot_of(group)
        if not keep:
            scores_of(group, slot)
        dp[...] = lax.dot_general(
            kv_all[group, 1].reshape(rows, HD), dost[...], nt, preferred_element_type=f32
        )

        def chunk(i, _):
            at = pl.ds(pl.multiple_of(i * CHUNK, CHUNK), CHUNK)
            probs = jnp.exp(sm[slot, at, :] - lse)
            pb[at, :] = probs.astype(bf16)
            ds_all[group, at, :] = (probs * (dp[at, :] - delta)).astype(bf16)
            return 0

        lax.fori_loop(0, chunks, chunk, 0, unroll=2)
        dv = jnp.dot(pb[...], dost[...], preferred_element_type=f32)
        dk = jnp.dot(ds_all[group], qst[...], preferred_element_type=f32) * scale
        for hh in range(H):
            part[group, hh % G, hh // G, 0] = dk[hh * qrow:(hh + 1) * qrow, :]
            part[group, hh % G, hh // G, 1] = dv[hh * qrow:(hh + 1) * qrow, :]
        sib_copy(group).start()

    def combine(group):
        sib_copy(group).wait_recv()
        for gg in range(KV):
            comb[group, gg] = (part[group, s, gg] + fromsib[group, gg]).astype(bf16)

    def combine_and_send(group):
        combine(group)
        for gg in range(KV):
            out_copy(group, gg, me).start()

    def grad_step(i, _):
        group = (c + i) % C
        fcopy(1, group, 1 - s).wait_recv()
        grads(group)
        combine_and_send(group)
        return 0

    lax.fori_loop(1, C, grad_step, 0)
    grads(c)
    combine(c)
    others = [(g + gg) % KV for gg in range(1, KV)]
    for gg in others:
        out_copy(c, gg, me).start()

    dqt = lax.dot_general(
        kv_all[:, 0].reshape(C * rows, HD), ds_all[...].reshape(C * rows, cols),
        (((0,), (0,)), ((), ())), preferred_element_type=f32,
    ) * scale
    for i in range(heads):
        dq_ref[:, i * HD:(i + 1) * HD] = dqt[:, i * rows:(i + 1) * rows].T.astype(bf16)

    own = part[c, s, g] + fromsib[c, g]

    def collect(gg):
        def step(i, total):
            src = ((c + i) % C) * KV + gg
            out_copy(c, gg, src).wait_recv()
            return total + recv[src].astype(f32)
        return step

    sums = lax.fori_loop(1, C, collect(g), own)
    mine = pl.ds(pl.multiple_of(g * HD, HD), HD)
    dk_ref[:, mine] = sums[0]
    dv_ref[:, mine] = sums[1]
    for gg in others:
        sums = lax.fori_loop(0, C, collect(gg), jnp.zeros_like(own))
        there = pl.ds(pl.multiple_of(gg * HD, HD), HD)
        dk_ref[:, there] = sums[0]
        dv_ref[:, there] = sums[1]

    def drain(i, _):
        group = (c + i) % C
        zcopy(0, c, group).wait_send()
        zcopy(1, c, group).wait_send()
        fcopy(0, group, s).wait_send()
        fcopy(1, group, s).wait_send()
        sib_copy(group).wait_send()
        for gg in range(KV):
            out_copy(group, gg, me).wait_send()
        return 0

    lax.fori_loop(1, C, drain, 0)
    sib_copy(c).wait_send()
    for gg in others:
        out_copy(c, gg, me).wait_send()


def shards(queries, key_rows, value_rows, saved_output, out_grad, block_pairs, piece_order):
    rows, width = queries.shape
    kv_width = key_rows.shape[1]
    heads = width // HD
    C = lax.axis_size("ctx")
    H = lax.axis_size("head")
    KV = kv_width // HD
    G = H // KV
    cols = rows * heads
    qrow = rows // H
    keep = C <= 4
    vmem = pl.BlockSpec(memory_space=pltpu.VMEM)
    dma = pltpu.SemaphoreType.DMA
    return pl.pallas_call(
        functools.partial(kernel, C, G, KV, keep),
        out_shape=(
            jax.ShapeDtypeStruct((rows, width), bf16),
            jax.ShapeDtypeStruct((qrow, kv_width), f32),
            jax.ShapeDtypeStruct((qrow, kv_width), f32),
        ),
        in_specs=[vmem] * 6 + [pl.BlockSpec(memory_space=pltpu.SMEM)],
        out_specs=(vmem, vmem, vmem),
        scratch_shapes=[
            pltpu.VMEM((cols, HD), bf16),
            pltpu.VMEM((cols, HD), bf16),
            pltpu.VMEM((C, 2, G, rows // G, HD), bf16),
            pltpu.VMEM((C if keep else 1, rows, cols), f32),
            pltpu.VMEM((rows, cols), f32),
            pltpu.VMEM((rows, cols), bf16),
            pltpu.VMEM((C, rows, cols), bf16),
            pltpu.VMEM((BLOCK, BLOCK), f32),
            pltpu.VMEM((C * rows // BLOCK, 1, cols), f32),
            pltpu.VMEM((C, G, KV, 2, qrow, HD), f32),
            pltpu.VMEM((C, KV, 2, qrow, HD), f32),
            pltpu.VMEM((C, KV, 2, qrow, HD), bf16),
            pltpu.VMEM((C * KV, 2, qrow, HD), bf16),
            dma((2 * C,)), dma((2 * C,)), dma((2 * C,)), dma((2 * C,)),
            dma((C,)), dma((C,)), dma((C * KV,)), dma((C * KV,)),
        ],
        compiler_params=pltpu.CompilerParams(
            collective_id=0, has_side_effects=True, vmem_limit_bytes=56 * 1024 * 1024
        ),
    )(queries, key_rows, value_rows, saved_output, out_grad, block_pairs, piece_order)


def solution(mesh):
    placed = (
        P(("rep", "ctx"), "head"),
        P(("rep", "ctx"), None),
        P(("rep", "ctx"), None),
        P(("rep", "ctx"), "head"),
        P(("rep", "ctx"), "head"),
        P(),
        P(),
    )
    return jax.shard_map(
        shards,
        mesh=mesh,
        in_specs=placed,
        out_specs=(
            P(("rep", "ctx"), "head"),
            P(("rep", "ctx", "head"), None),
            P(("rep", "ctx", "head"), None),
        ),
        check_vma=False,
    )
```

profile of v0, /device:TPU:12, one launch (start us, length us, event | category | flops | bytes accessed | tf_op | source)
XLA Modules:
  0.0 44.0 jit_solution(14134883428250909844)
XLA Ops:
  0.6 1.4 %copy.10.pairs_ref = s32[80,2]{1,0:T(8,128)} copy(s32[80,2]{0,1:T(2,128)} %param.12) | data formatting | bytes 1280 | tf_op args[5]
  2.0 38.7 %shard_map.94 = (bf16[512,256]{1,0:T(8,128)(2,1)}, f32[128,256]{1,0:T(8,128)}, f32[128,256]{1,0:T(8,128)}) custom-call(bf16[512,256]{1,0:T(8,128)(2,1)} %q_ref.1, bf16[512,256]{1,0:T(8,128)(2,1)} %k_ref.1, bf16[512,256]{1,0:T(8,128)(2,1)} %v_ref.1, bf16[512,256]{1,0:T(8,128)(2,1)} %o_ref.1, bf16[512,256]{1,0:T(8,128)(2,1)} %g_ref.1, ...), custom_call_target="tpu_custom_call" | custom-call | tf_op jit(solution)/shard_map/pallas_call | solution.py:299
  40.7 0.0 copy-start.1
  40.7 1.7 %copy.14 = bf16[512,256]{1,0:T(8,128)(2,1)} copy(bf16[512,256]{1,0:T(8,128)(2,1)} %get-tuple-element.6) | data formatting | bytes 524288
  42.4 0.0 copy-done.1
  42.4 0.0 copy-start
  42.4 0.7 %copy.15 = f32[128,256]{1,0:T(8,128)} copy(f32[128,256]{1,0:T(8,128)S(1)} %copy-done.1) | data formatting | bytes 262144
  43.1 0.3 copy-done
  43.4 0.7 %copy.16 = f32[128,256]{1,0:T(8,128)} copy(f32[128,256]{1,0:T(8,128)S(1)} %copy-done) | data formatting | bytes 262144
Async XLA Ops:
  40.7 1.7 %copy-start.1 = (f32[128,256]{1,0:T(8,128)S(1)}, f32[128,256]{1,0:T(8,128)}, u32[]{:S(2)}) copy-start(f32[128,256]{1,0:T(8,128)} %get-tuple-element.7) | copy-start | bytes 393220
  42.4 1.0 %copy-start = (f32[128,256]{1,0:T(8,128)S(1)}, f32[128,256]{1,0:T(8,128)}, u32[]{:S(2)}) copy-start(f32[128,256]{1,0:T(8,128)} %get-tuple-element.8) | copy-start | bytes 393220
where the time goes:
time: 44.2 us; the launch traced here: 44 us
  Pallas kernels  38.7 us (88%)
  local copies, waits for them, and re-layouts  4.7 us (11%)
  between operations  0.65 us (1%)
    pallas_call x1, Pallas kernels, shards(): pl.pallas_call(functools.partial(kernel, C, G, KV, keep), out_shape=(jax....  38.7 us
    unnamed x8, local copies, waits for them, and re-layouts  4.7 us

commit v1 on v0

--- a/solution.py
+++ b/solution.py
@@ -57,6 +57,44 @@
         kv_all[c, 0, i] = k_ref[i * half:(i + 1) * half, gcol]
         kv_all[c, 1, i] = v_ref[i * half:(i + 1) * half, gcol]
 
+    for i in range(heads):
+        qst[i * rows:(i + 1) * rows, :] = q_ref[:, i * HD:(i + 1) * HD]
+        dost[i * rows:(i + 1) * rows, :] = g_ref[:, i * HD:(i + 1) * HD]
+
+    per_piece = piece // BLOCK
+    slots = C * blocks
+
+    def stored_blocks(shape, dim, first):
+        at = lax.broadcasted_iota(jnp.int32, shape, dim)
+        ids = jnp.zeros(shape, jnp.int32)
+        for i in range(shape[dim] // per_piece):
+            ids = jnp.where(
+                at // per_piece == i, order_ref[first + i] * per_piece + at % per_piece, ids
+            )
+        return ids
+
+    lane = lax.broadcasted_iota(jnp.int32, (1, cols), 1) % rows
+    qblk = (
+        jnp.where(lane < piece, order_ref[2 * c], order_ref[2 * c + 1]) * per_piece
+        + (lane % piece) // BLOCK
+    )
+    kblk = stored_blocks((slots, 1), 0, 0)
+    own_q = stored_blocks((blocks, 1), 0, 2 * c)
+    hits_q = (own_q == pairs_ref[0:1, :]).astype(f32)
+    hits_k = (kblk == pairs_ref[1:2, :]).astype(f32)
+    nt = (((1,), (1,)), ((), ()))
+    table = lax.dot_general(hits_k, hits_q, nt, preferred_element_type=f32)
+    live = jnp.concatenate(
+        [jnp.broadcast_to(table[:, i:i + 1], (slots, BLOCK)) for i in range(blocks)] * heads, axis=1
+    )
+    thr[...] = jnp.where(
+        live > 0.5, jnp.where(kblk < qblk, far, jnp.where(kblk == qblk, 0.0, -far)), -far
+    ).reshape(slots, 1, cols)
+    diff[...] = (
+        lax.broadcasted_iota(jnp.int32, (BLOCK, BLOCK), 0)
+        - lax.broadcasted_iota(jnp.int32, (BLOCK, BLOCK), 1)
+    ).astype(f32)
+
     pl.semaphore_wait(barrier, KV * C)
 
     def zcopy(kind, group, to):
@@ -78,38 +116,6 @@
             zcopy(kind, c, (c + i) % C).start()
             return 0
         lax.fori_loop(1, C, send, 0)
-
-    for i in range(heads):
-        qst[i * rows:(i + 1) * rows, :] = q_ref[:, i * HD:(i + 1) * HD]
-        dost[i * rows:(i + 1) * rows, :] = g_ref[:, i * HD:(i + 1) * HD]
-
-    lane = lax.broadcasted_iota(jnp.int32, (1, cols), 1) % rows
-    qblk = (
-        jnp.where(lane < piece, order_ref[2 * c], order_ref[2 * c + 1]) * (piece // BLOCK)
-        + (lane % piece) // BLOCK
-    )
-    slots = C * blocks
-    per_piece = piece // BLOCK
-    slot_row = lax.broadcasted_iota(jnp.int32, (1, slots), 1)
-    slot_col = lax.broadcasted_iota(jnp.int32, (slots, 1), 0)
-    kblk_row = jnp.zeros((1, slots), jnp.int32)
-    kblk_col = jnp.zeros((slots, 1), jnp.int32)
-    for i in range(2 * C):
-        first = order_ref[i] * per_piece
-        kblk_row = jnp.where(slot_row // per_piece == i, first + slot_row % per_piece, kblk_row)
-        kblk_col = jnp.where(slot_col // per_piece == i, first + slot_col % per_piece, kblk_col)
-    hits_q = (pairs_ref[:, 0:1] == qblk).astype(f32)
-    hits_k = (pairs_ref[:, 1:2] == kblk_row).astype(f32)
-    live = lax.dot_general(hits_k, hits_q, (((0,), (0,)), ((), ())), preferred_element_type=f32)
-    thr[...] = jnp.where(
-        live > 0.5,
-        jnp.where(kblk_col < qblk, far, jnp.where(kblk_col == qblk, 0.0, -far)),
-        -far,
-    ).reshape(slots, 1, cols)
-    diff[...] = (
-        lax.broadcasted_iota(jnp.int32, (BLOCK, BLOCK), 0)
-        - lax.broadcasted_iota(jnp.int32, (BLOCK, BLOCK), 1)
-    ).astype(f32)
 
     delta_parts = []
     for i in range(heads):
@@ -120,7 +126,6 @@
 
     per_block = BLOCK // CHUNK
     chunks = rows // CHUNK
-    nt = (((1,), (1,)), ((), ()))
 
     def scores_of(group, slot):
         sm[slot] = lax.dot_general(
@@ -169,31 +174,52 @@
     run_max, run_sum = lax.fori_loop(1, C, gather_step, carry)
     lse = run_max + jnp.log(run_sum)
 
-    def forward_values(i, _):
-        group = (c - i + C) % C
-        zcopy(1, group, c).wait_recv()
-        fcopy(1, group, s).start()
-        return 0
-
-    lax.fori_loop(1, C, forward_values, 0)
-
-    def sib_copy(group):
+    def sib_copy(kind, group):
         return pltpu.make_async_remote_copy(
-            src_ref=part.at[group, 1 - s], dst_ref=fromsib.at[group],
-            send_sem=sibsend.at[group], recv_sem=sibrecv.at[group],
+            src_ref=part.at[kind, group, 1 - s], dst_ref=fromsib.at[kind, group],
+            send_sem=sibsend.at[kind * C + group], recv_sem=sibrecv.at[kind * C + group],
             device_id={"head": sib}, device_id_type=MESH,
         )
 
-    def out_copy(group, gg, src):
+    def out_copy(kind, group, gg, src):
         return pltpu.make_async_remote_copy(
-            src_ref=comb.at[group, gg], dst_ref=recv.at[src],
-            send_sem=rsend.at[group * KV + gg], recv_sem=rrecv.at[src],
+            src_ref=comb.at[kind, group, gg], dst_ref=recv.at[kind, src],
+            send_sem=rsend.at[(kind * C + group) * KV + gg],
+            recv_sem=rrecv.at[kind * C * KV + src],
             device_id={"ctx": group, "head": gg * G + s}, device_id_type=MESH,
         )
 
     me = c * KV + g
-
-    def grads(group):
+    others = [(g + gg) % KV for gg in range(1, KV)]
+
+    def share(kind, group, value):
+        for hh in range(H):
+            part[kind, group, hh % G, hh // G] = value[hh * qrow:(hh + 1) * qrow, :]
+        sib_copy(kind, group).start()
+
+    def combine(kind, group, own=False):
+        sib_copy(kind, group).wait_recv()
+        for gg in range(KV):
+            comb[kind, group, gg] = (part[kind, group, s, gg] + fromsib[kind, group, gg]).astype(bf16)
+        for gg in others if own else range(KV):
+            out_copy(kind, group, gg, me).start()
+
+    def value_part(group):
+        slot = slot_of(group)
+        if not keep:
+            scores_of(group, slot)
+
+        def chunk(i, _):
+            at = pl.ds(pl.multiple_of(i * CHUNK, CHUNK), CHUNK)
+            probs = jnp.exp(sm[slot, at, :] - lse)
+            sm[slot, at, :] = probs
+            pb[at, :] = probs.astype(bf16)
+            return 0
+
+        lax.fori_loop(0, chunks, chunk, 0, unroll=2)
+        share(1, group, jnp.dot(pb[...], dost[...], preferred_element_type=f32))
+
+    def key_part(group):
         slot = slot_of(group)
         if not keep:
             scores_of(group, slot)
@@ -203,42 +229,51 @@
 
         def chunk(i, _):
             at = pl.ds(pl.multiple_of(i * CHUNK, CHUNK), CHUNK)
-            probs = jnp.exp(sm[slot, at, :] - lse)
-            pb[at, :] = probs.astype(bf16)
+            probs = sm[slot, at, :] if keep else jnp.exp(sm[slot, at, :] - lse)
             ds_all[group, at, :] = (probs * (dp[at, :] - delta)).astype(bf16)
             return 0
 
         lax.fori_loop(0, chunks, chunk, 0, unroll=2)
-        dv = jnp.dot(pb[...], dost[...], preferred_element_type=f32)
-        dk = jnp.dot(ds_all[group], qst[...], preferred_element_type=f32) * scale
-        for hh in range(H):
-            part[group, hh % G, hh // G, 0] = dk[hh * qrow:(hh + 1) * qrow, :]
-            part[group, hh % G, hh // G, 1] = dv[hh * qrow:(hh + 1) * qrow, :]
-        sib_copy(group).start()
-
-    def combine(group):
-        sib_copy(group).wait_recv()
-        for gg in range(KV):
-            comb[group, gg] = (part[group, s, gg] + fromsib[group, gg]).astype(bf16)
-
-    def combine_and_send(group):
-        combine(group)
-        for gg in range(KV):
-            out_copy(group, gg, me).start()
-
-    def grad_step(i, _):
+        share(0, group, jnp.dot(ds_all[group], qst[...], preferred_element_type=f32) * scale)
+
+    value_part(c)
+
+    def value_step(i, _):
+        arrived = (c - i + C) % C
+        value_part((c + i) % C)
+
+        @pl.when(i == 1)
+        def _():
+            combine(1, c, own=True)
+
+        @pl.when(i > 1)
+        def _():
+            combine(1, (c + i - 1) % C)
+
+        zcopy(1, arrived, c).wait_recv()
+        fcopy(1, arrived, s).start()
+        return 0
+
+    lax.fori_loop(1, C, value_step, 0)
+
+    def key_step(i, _):
         group = (c + i) % C
         fcopy(1, group, 1 - s).wait_recv()
-        grads(group)
-        combine_and_send(group)
+        key_part(group)
+
+        @pl.when(i == 1)
+        def _():
+            combine(1, (c + C - 1) % C)
+
+        @pl.when(i > 1)
+        def _():
+            combine(0, (c + i - 1) % C)
+
         return 0
 
-    lax.fori_loop(1, C, grad_step, 0)
-    grads(c)
-    combine(c)
-    others = [(g + gg) % KV for gg in range(1, KV)]
-    for gg in others:
-        out_copy(c, gg, me).start()
+    lax.fori_loop(1, C, key_step, 0)
+    key_part(c)
+    combine(0, (c + C - 1) % C)
 
     dqt = lax.dot_general(
         kv_all[:, 0].reshape(C * rows, HD), ds_all[...].reshape(C * rows, cols),
@@ -247,40 +282,38 @@
     for i in range(heads):
         dq_ref[:, i * HD:(i + 1) * HD] = dqt[:, i * rows:(i + 1) * rows].T.astype(bf16)
 
-    own = part[c, s, g] + fromsib[c, g]
-
-    def collect(gg):
-        def step(i, total):
-            src = ((c + i) % C) * KV + gg
-            out_copy(c, gg, src).wait_recv()
-            return total + recv[src].astype(f32)
-        return step
-
-    sums = lax.fori_loop(1, C, collect(g), own)
-    mine = pl.ds(pl.multiple_of(g * HD, HD), HD)
-    dk_ref[:, mine] = sums[0]
-    dv_ref[:, mine] = sums[1]
-    for gg in others:
-        sums = lax.fori_loop(0, C, collect(gg), jnp.zeros_like(own))
-        there = pl.ds(pl.multiple_of(gg * HD, HD), HD)
-        dk_ref[:, there] = sums[0]
-        dv_ref[:, there] = sums[1]
+    combine(0, c, own=True)
+
+    for kind, out_ref in ((1, dv_ref), (0, dk_ref)):
+        own = part[kind, c, s, g] + fromsib[kind, c, g]
+
+        def collect(gg, kind=kind):
+            def step(i, total):
+                src = ((c + i) % C) * KV + gg
+                out_copy(kind, c, gg, src).wait_recv()
+                return total + recv[kind, src].astype(f32)
+            return step
+
+        out_ref[:, gcol] = lax.fori_loop(1, C, collect(g), own)
+        for gg in others:
+            there = pl.ds(pl.multiple_of(gg * HD, HD), HD)
+            out_ref[:, there] = lax.fori_loop(0, C, collect(gg), jnp.zeros_like(own))
 
     def drain(i, _):
         group = (c + i) % C
-        zcopy(0, c, group).wait_send()
-        zcopy(1, c, group).wait_send()
-        fcopy(0, group, s).wait_send()
-        fcopy(1, group, s).wait_send()
-        sib_copy(group).wait_send()
-        for gg in range(KV):
-            out_copy(group, gg, me).wait_send()
+        for kind in range(2):
+            zcopy(kind, c, group).wait_send()
+            fcopy(kind, group, s).wait_send()
+            sib_copy(kind, group).wait_send()
+            for gg in range(KV):
+                out_copy(kind, group, gg, me).wait_send()
         return 0
 
     lax.fori_loop(1, C, drain, 0)
-    sib_copy(c).wait_send()
-    for gg in others:
-        out_copy(c, gg, me).wait_send()
+    for kind in range(2):
+        sib_copy(kind, c).wait_send()
+        for gg in others:
+            out_copy(kind, c, gg, me).wait_send()
 
 
 def shards(queries, key_rows, value_rows, saved_output, out_grad, block_pairs, piece_order):
@@ -315,17 +348,17 @@
             pltpu.VMEM((C, rows, cols), bf16),
             pltpu.VMEM((BLOCK, BLOCK), f32),
             pltpu.VMEM((C * rows // BLOCK, 1, cols), f32),
-            pltpu.VMEM((C, G, KV, 2, qrow, HD), f32),
-            pltpu.VMEM((C, KV, 2, qrow, HD), f32),
-            pltpu.VMEM((C, KV, 2, qrow, HD), bf16),
-            pltpu.VMEM((C * KV, 2, qrow, HD), bf16),
+            pltpu.VMEM((2, C, G, KV, qrow, HD), f32),
+            pltpu.VMEM((2, C, KV, qrow, HD), f32),
+            pltpu.VMEM((2, C, KV, qrow, HD), bf16),
+            pltpu.VMEM((2, C * KV, qrow, HD), bf16),
             dma((2 * C,)), dma((2 * C,)), dma((2 * C,)), dma((2 * C,)),
-            dma((C,)), dma((C,)), dma((C * KV,)), dma((C * KV,)),
+            dma((2 * C,)), dma((2 * C,)), dma((2 * C * KV,)), dma((2 * C * KV,)),
         ],
         compiler_params=pltpu.CompilerParams(
             collective_id=0, has_side_effects=True, vmem_limit_bytes=56 * 1024 * 1024
         ),
-    )(queries, key_rows, value_rows, saved_output, out_grad, block_pairs, piece_order)
+    )(queries, key_rows, value_rows, saved_output, out_grad, block_pairs.T, piece_order)
 
 
 def solution(mesh):

time: 44.2 us -> 42.4 us (0.959)
  the two profiles are of different devices: /device:TPU:12 before, /device:TPU:0 now
where the time goes in v1:
time: 42.4 us; the launch traced here: 42.2 us
  Pallas kernels  38.2 us (90%)
  local copies, waits for them, and re-layouts  3.31 us (8%)
  between operations  0.65 us (2%)
    pallas_call x1, Pallas kernels, shards(): pl.pallas_call(functools.partial(kernel, C, G, KV, keep), out_shape=(jax....  38.2 us
    unnamed x7, local copies, waits for them, and re-layouts  3.31 us

profile of v1, /device:TPU:0, one launch (start us, length us, event | category | flops | bytes accessed | tf_op | source)
XLA Modules:
  0.0 42.2 jit_solution(3400755551175987464)
XLA Ops:
  0.6 38.2 %shard_map.94 = (bf16[512,256]{1,0:T(8,128)(2,1)}, f32[128,256]{1,0:T(8,128)}, f32[128,256]{1,0:T(8,128)}) custom-call(bf16[512,256]{1,0:T(8,128)(2,1)} %q_ref.1, bf16[512,256]{1,0:T(8,128)(2,1)} %k_ref.1, bf16[512,256]{1,0:T(8,128)(2,1)} %v_ref.1, bf16[512,256]{1,0:T(8,128)(2,1)} %o_ref.1, bf16[512,256]{1,0:T(8,128)(2,1)} %g_ref.1, s32[2,80]{1,0:T(2,128)} %bitcast.1, ...), custom_call_target="tpu_custom_call" | custom-call | tf_op jit(solution)/shard_map/pallas_call | solution.py:332
  38.9 0.0 copy-start.1
  38.9 1.7 %copy.13 = bf16[512,256]{1,0:T(8,128)(2,1)} copy(bf16[512,256]{1,0:T(8,128)(2,1)} %get-tuple-element.6) | data formatting | bytes 524288
  40.6 0.0 copy-done.1
  40.6 0.0 copy-start
  40.6 0.7 %copy.14 = f32[128,256]{1,0:T(8,128)} copy(f32[128,256]{1,0:T(8,128)S(1)} %copy-done.1) | data formatting | bytes 262144
  41.2 0.3 copy-done
  41.5 0.7 %copy.15 = f32[128,256]{1,0:T(8,128)} copy(f32[128,256]{1,0:T(8,128)S(1)} %copy-done) | data formatting | bytes 262144
Async XLA Ops:
  38.9 1.7 %copy-start.1 = (f32[128,256]{1,0:T(8,128)S(1)}, f32[128,256]{1,0:T(8,128)}, u32[]{:S(2)}) copy-start(f32[128,256]{1,0:T(8,128)} %get-tuple-element.7) | copy-start | bytes 393220
  40.6 1.0 %copy-start = (f32[128,256]{1,0:T(8,128)S(1)}, f32[128,256]{1,0:T(8,128)}, u32[]{:S(2)}) copy-start(f32[128,256]{1,0:T(8,128)} %get-tuple-element.8) | copy-start | bytes 393220

commit v2 on v1

--- a/solution.py
+++ b/solution.py
@@ -9,7 +9,7 @@
 
 HD = 128
 BLOCK = 128
-CHUNK = 32
+CHUNK = 64
 
 very_low = -1e30
 far = 1e9
@@ -164,13 +164,21 @@
 
     carry = stats(c, (jnp.full((1, cols), very_low, f32), jnp.zeros((1, cols), f32)))
 
+    def pass_on(kind, group):
+        zcopy(kind, group, c).wait_recv()
+        fcopy(kind, group, s).start()
+
     def gather_step(i, carry):
         group = (c - i + C) % C
-        zcopy(0, group, c).wait_recv()
-        fcopy(0, group, s).start()
+
+        @pl.when(i < C - 1)
+        def _():
+            pass_on(0, (c - i - 1 + C) % C)
+
         fcopy(0, group, 1 - s).wait_recv()
         return stats(group, carry)
 
+    pass_on(0, (c - 1 + C) % C)
     run_max, run_sum = lax.fori_loop(1, C, gather_step, carry)
     lse = run_max + jnp.log(run_sum)
 
@@ -250,8 +258,7 @@
         def _():
             combine(1, (c + i - 1) % C)
 
-        zcopy(1, arrived, c).wait_recv()
-        fcopy(1, arrived, s).start()
+        pass_on(1, arrived)
         return 0
 
     lax.fori_loop(1, C, value_step, 0)
@@ -314,6 +321,12 @@
         sib_copy(kind, c).wait_send()
         for gg in others:
             out_copy(kind, c, gg, me).wait_send()
+
+
+def hand_over(dq_in, dk_in, dv_in, dq_ref, dk_ref, dv_ref):
+    dq_ref[...] = dq_in[...]
+    dk_ref[...] = dk_in[...]
+    dv_ref[...] = dv_in[...]
 
 
 def shards(queries, key_rows, value_rows, saved_output, out_grad, block_pairs, piece_order):
@@ -329,7 +342,7 @@
     keep = C <= 4
     vmem = pl.BlockSpec(memory_space=pltpu.VMEM)
     dma = pltpu.SemaphoreType.DMA
-    return pl.pallas_call(
+    grads = pl.pallas_call(
         functools.partial(kernel, C, G, KV, keep),
         out_shape=(
             jax.ShapeDtypeStruct((rows, width), bf16),
@@ -359,6 +372,12 @@
             collective_id=0, has_side_effects=True, vmem_limit_bytes=56 * 1024 * 1024
         ),
     )(queries, key_rows, value_rows, saved_output, out_grad, block_pairs.T, piece_order)
+    return pl.pallas_call(
+        hand_over,
+        out_shape=tuple(jax.ShapeDtypeStruct(x.shape, x.dtype) for x in grads),
+        in_specs=[vmem] * 3,
+        out_specs=(vmem,) * 3,
+    )(*grads)
 
 
 def solution(mesh):

time: 42.4 us -> 39.3 us (0.927)
  local copies, waits for them, and re-layouts: 3.31 us -> 0 us
    unnamed x7 -> x0, local copies, waits for them, and re-layouts: 3.31 us -> none
    pallas_call x0 -> x1, Pallas kernels: none -> 1.84 us  [shards(): pl.pallas_call(hand_over, out_shape=tuple((jax.ShapeDtypeStruct(x.shape,...]
    pallas_call x1, Pallas kernels: 38.2 us -> 36.7 us  [shards(): pl.pallas_call(functools.partial(kernel, C, G, KV, keep), out_shape=(jax....]
where the time goes in v2:
time: 39.3 us; the launch traced here: 39.1 us
  Pallas kernels  38.5 us (98%)
  between operations  0.64 us (2%)
    pallas_call x1, Pallas kernels, shards(): pl.pallas_call(functools.partial(kernel, C, G, KV, keep), out_shape=(jax....  36.7 us
    pallas_call x1, Pallas kernels, shards(): pl.pallas_call(hand_over, out_shape=tuple((jax.ShapeDtypeStruct(x.shape,...  1.84 us

profile of v2, /device:TPU:0, one launch (start us, length us, event | category | flops | bytes accessed | tf_op | source)
XLA Modules:
  0.0 39.1 jit_solution(11879344714728520751)
XLA Ops:
  0.6 36.7 %shard_map.94 = (bf16[512,256]{1,0:T(8,128)(2,1)}, f32[128,256]{1,0:T(8,128)}, f32[128,256]{1,0:T(8,128)}) custom-call(bf16[512,256]{1,0:T(8,128)(2,1)} %q_ref.1, bf16[512,256]{1,0:T(8,128)(2,1)} %k_ref.1, bf16[512,256]{1,0:T(8,128)(2,1)} %v_ref.1, bf16[512,256]{1,0:T(8,128)(2,1)} %o_ref.1, bf16[512,256]{1,0:T(8,128)(2,1)} %g_ref.1, s32[2,80]{1,0:T(2,128)} %bitcast.1, ...), custom_call_target="tpu_custom_call" | custom-call | tf_op jit(solution)/shard_map/pallas_call | solution.py:345
  37.3 1.8 %shard_map.95 = (bf16[512,256]{1,0:T(8,128)(2,1)}, f32[128,256]{1,0:T(8,128)}, f32[128,256]{1,0:T(8,128)}) custom-call(bf16[512,256]{1,0:T(8,128)(2,1)} %get-tuple-element.6.dq_in, f32[128,256]{1,0:T(8,128)} %get-tuple-element.7.dk_in, f32[128,256]{1,0:T(8,128)} %get-tuple-element.8.dv_in), custom_call_target="tpu_custom_call" | custom-call | tf_op jit(solution)/shard_map/pallas_call | solution.py:375
